TPU v7x, 256 devices: a whole 4x4x8 slice. The times are simulated.
256 devices in a mesh: row: 16 (over z_hi, y), col: 16 (over z_lo, x, core).
Axes of the slice: x: 4, y: 4, z: 8 (z_hi: 4, z_lo: 2; z = z_hi * 2 + z_lo), core: 2. Of those that a mesh axis runs over, the one named last changes fastest.
Arguments:
- a11: float32 [256, 256], replicated, as said below
- linv11: float32 [256, 256], replicated, as said below
- a21: float32 [16384, 256], P(('row', 'col')), may hold values from -6 to 6
- l21: float32 [16384, 256], P(('row', 'col')), may hold values from -0.4 to 0.4
- a22: float32 [16384, 16384], P('row', 'col'), may hold values from -6 to 6
Outputs:
- diag_block: float32 [256, 256], replicated
- panel: float32 [16384, 256], P(('row', 'col'))
- trailing: float32 [16384, 16384], P('row', 'col')
Inputs may be any that keep to these rules, and one draw needn't show every extreme that they name: `a11`: symmetric. `linv11`: lower triangular with a positive diagonal.
All inputs are finite; a program needn't handle non-finite values.
Results may differ from a plain program's by a relative error of at most 0.00005.
Values sent between devices are 32-bit elements; how exact they have to be, the bound alone decides.
A program may use at most 64 MiB of HBM per device.

v0:
```python
import jax
import jax.numpy as jnp
from jax import lax
from jax.sharding import PartitionSpec as P


def spread(value, axis, source):
    kept = jnp.where(lax.axis_index(axis) == source, value, 0).astype(value.dtype)
    return lax.psum(kept, axis)


def mult(a, b):
    return jnp.dot(a, b, precision=lax.Precision.HIGHEST, preferred_element_type=jnp.float32)


def body(a11, linv11, a21, l21, a22):
    width = a21.shape[1]
    diag_block = mult(mult(linv11, a11), linv11.T)
    correction = 0.5 * mult(l21, diag_block)
    half = mult(a21, linv11.T) - correction
    panel = half - correction
    packed = jnp.concatenate([half, l21], axis=1)
    n_row = lax.axis_size("row")
    n_col = lax.axis_size("col")
    groups = n_row // n_col
    mine = lax.all_gather(packed, "col", axis=0, tiled=True)
    col_index = lax.axis_index("col")
    parts = spread(mine, "row", col_index * groups + 0)
    flipped = jnp.concatenate([parts[:, width:], parts[:, :width]], axis=1)
    trailing = a22 - mult(mine, flipped.T)
    return (diag_block, panel, trailing)


def solution(mesh):
    return jax.shard_map(
        body,
        mesh=mesh,
        in_specs=(P(), P(), P(("row", "col"), None), P(("row", "col"), None), P("row", "col")),
        out_specs=(P(), P(("row", "col"), None), P("row", "col")),
        check_vma=False,
    )
```

profile of v0, /device:TPU:4, one launch (start us, length us, event | category | flops | bytes accessed | tf_op | source)
XLA Modules:
  0.0 254.2 jit_solution(17430890461005125020)
XLA Ops:
  7.2 0.0 copy-start
  7.2 0.0 copy-start.3
  7.2 0.0 all-gather.2.cloned.1.call-start
  7.2 0.9 copy-done
  8.1 1.3 fusion.7
  9.5 0.4 fusion.8
  9.9 0.0 copy-start.2
  9.9 1.2 fusion.3
  11.1 1.8 fusion.6
  12.9 0.0 copy-done.3
  12.9 0.7 pad_maximum_fusion
  13.6 0.0 all-gather.2.cloned.1.call-update
  13.6 0.0 all-reduce.2.cloned.1.call-start
  13.7 38.5 %all-gather.2.cloned.1.call-done = f32[1024,512]{1,0:T(8,128)} async-done(((f32[64,512]{1,0:T(8,128)}), f32[1024,512]{1,0:T(8,128)}) %all-gather.2.cloned.1.call-update) | async-done | bytes 2097168 | tf_op jit(solution)/shard_map/all_gather | solution.py:26
  52.2 1.5 broadcast_select_fusion
  53.7 0.0 copy-done.2
  53.7 0.0 all-reduce.2.cloned.1.call-update
  53.7 0.0 copy-start.1
  53.7 182.1 %all-reduce.2.cloned.1.call-done = f32[1024,512]{1,0:T(8,128)} async-done(((f32[1024,512]{1,0:T(8,128)}), f32[1024,512]{1,0:T(8,128)}) %all-reduce.2.cloned.1.call-update) | async-done | bytes 2097168 | tf_op jit(solution)/shard_map/psum | solution.py:9
  235.8 1.7 fusion.5
  237.5 0.0 copy-done.1
  237.5 9.9 %convolution_subtract_fusion = f32[1024,1024]{1,0:T(8,128)} fusion(f32[1024,1024]{1,0:T(8,128)} %param.9, f32[1024,512]{1,0:T(8,128)S(1)} %copy-done.1, f32[1024,256]{1,0:T(8,128)S(1)} %get-tuple-element.4, f32[1024,256]{1,0:T(8,128)S(1)} %get-tuple-element.3), kind=kOutput, calls=%fused_computation | convolution fusion | flops 6444023808 | bytes 12582912 | tf_op jit(solution)/shard_map/dot_general | solution.py:13
Async XLA Ops:
  7.2 1.0 copy-start
  7.2 5.7 %copy-start.3 = (f32[64,256]{1,0:T(8,128)S(1)}, f32[64,256]{1,0:T(8,128)}, u32[]{:S(2)}) copy-start(f32[64,256]{1,0:T(8,128)} %param.8) | copy-start | bytes 196612
  7.2 45.0 %all-gather.2.cloned.1.call-start = ((), (), s32[]{:S(2)}) async-start(), calls=%async_computation | async-start | bytes 2228224 | tf_op jit(solution)/shard_map/all_gather | solution.py:26
  9.9 43.8 %copy-start.2 = (f32[256,256]{1,0:T(8,128)}, f32[256,256]{1,0:T(8,128)S(1)}, u32[]{:S(2)}) copy-start(f32[256,256]{1,0:T(8,128)S(1)} %fusion.8) | copy-start | bytes 786436
  13.6 222.2 %all-reduce.2.cloned.1.call-start = ((), (), s32[]{:S(2)}) async-start(), calls=%async_computation.1 | async-start | bytes 4194304 | tf_op jit(solution)/shard_map/psum | solution.py:9
  53.7 183.8 %copy-start.1 = (f32[1024,512]{1,0:T(8,128)S(1)}, f32[1024,512]{1,0:T(8,128)}, u32[]{:S(2)}) copy-start(f32[1024,512]{1,0:T(8,128)} %all-gather.2.cloned.1.call-done) | copy-start | bytes 6291460
Sparse Core Ops, SparseCore 0:
  13.7 38.3 all-gather.1
  55.4 180.3 all-reduce.1
where the time goes:
time: 255 us; the launch traced here: 254 us
  waiting for transfers between devices  221 us (87%)
  matrix products  14.6 us (6%)
  between operations  14.1 us (6%)
  local copies, waits for them, and re-layouts  2.58 us (1%)
    psum x1, waiting for transfers between devices, spread(): return lax.psum(kept, axis)  182 us
    all_gather x1, waiting for transfers between devices, body(): mine = lax.all_gather(packed, 'col', axis=0, tiled=True)  38.5 us
    dot_general x5, matrix products, mult(): jnp.dot(a, b, precision=lax.Precision.HIGHEST, preferred_element_type=jnp...  14.6 us
  transfers between devices with their start and end apart: 2, of which 2 were waited for; matrix products, arithmetic and copies ran while one was open for 0% of the time, Pallas kernels for 0%

commit v1 on v0

--- a/solution.py
+++ b/solution.py
@@ -6,7 +6,7 @@
 
 def spread(value, axis, source):
     kept = jnp.where(lax.axis_index(axis) == source, value, 0).astype(value.dtype)
-    return lax.psum(kept, axis)
+    return jnp.sum(lax.all_gather(kept, axis), axis=0)
 
 
 def mult(a, b):

time: 255 us -> 461 us (1.81)
  waiting for transfers between devices: 221 us -> 414 us
  other arithmetic: 2.21 us -> 14.9 us
    all_gather x0 -> x1, waiting for transfers between devices: none -> 375 us  [spread(): return jnp.sum(lax.all_gather(kept, axis), axis=0)]
    psum x1 -> x0, waiting for transfers between devices: 182 us -> none  [spread(): return lax.psum(kept, axis)]
    reduce_sum x0 -> x1, other arithmetic: none -> 12.7 us  [spread(): return jnp.sum(lax.all_gather(kept, axis), axis=0)]
where the time goes in v1:
time: 461 us; the launch traced here: 460 us
  waiting for transfers between devices  414 us (90%)
  other arithmetic  14.9 us (3%)
  matrix products  14.6 us (3%)
  between operations  14.1 us (3%)
    all_gather x1, waiting for transfers between devices, spread(): return jnp.sum(lax.all_gather(kept, axis), axis=0)  375 us
    all_gather x1, waiting for transfers between devices, body(): mine = lax.all_gather(packed, 'col', axis=0, tiled=True)  38.5 us
    dot_general x5, matrix products, mult(): jnp.dot(a, b, precision=lax.Precision.HIGHEST, preferred_element_type=jnp...  14.6 us
    reduce_sum x1, other arithmetic, spread(): return jnp.sum(lax.all_gather(kept, axis), axis=0)  12.7 us
  transfers between devices with their start and end apart: 2, of which 2 were waited for; matrix products, arithmetic and copies ran while one was open for 0% of the time, Pallas kernels for 0%

profile of v1, /device:TPU:4, one launch (start us, length us, event | category | flops | bytes accessed | tf_op | source)
XLA Modules:
  0.0 460.2 jit_solution(10071502147895484908)
XLA Ops:
  7.2 0.0 copy-start
  7.2 0.0 copy-start.3
  7.2 0.0 all-gather.4.cloned.1.call-start
  7.2 0.9 copy-done
  8.1 1.3 fusion.7
  9.5 0.4 fusion.8
  9.9 0.0 copy-start.2
  9.9 1.2 fusion.3
  11.1 1.8 fusion.6
  12.9 0.0 copy-done.3
  12.9 0.7 pad_maximum_fusion
  13.6 0.0 all-gather.4.cloned.1.call-update
  13.6 0.0 all-gather.6.cloned.1.call-start
  13.7 38.5 %all-gather.4.cloned.1.call-done = f32[1024,512]{1,0:T(8,128)} async-done(((f32[64,512]{1,0:T(8,128)}), f32[1024,512]{1,0:T(8,128)}) %all-gather.4.cloned.1.call-update) | async-done | bytes 2097168 | tf_op jit(solution)/shard_map/all_gather | solution.py:26
  52.2 1.5 broadcast_select_fusion
  53.7 0.0 copy-done.2
  53.7 0.0 all-gather.6.cloned.1.call-update
  53.7 375.5 %all-gather.6.cloned.1.call-done = f32[16384,512]{1,0:T(8,128)} async-done(((f32[1024,512]{1,0:T(8,128)}), f32[16384,512]{1,0:T(8,128)}) %all-gather.6.cloned.1.call-update) | async-done | bytes 33554448 | tf_op jit(solution)/shard_map/all_gather | solution.py:9
  429.2 12.7 %reduce_sum.9 = f32[1024,512]{1,0:T(8,128)S(1)} reduce(f32[16,1024,512]{2,1,0:T(8,128)} %bitcast.12, f32[]{:T(128)} %constant.12.clone.1), dimensions={0}, to_apply=%region_0.1 | reduce | flops 7864320 | bytes 35651588 | tf_op jit(solution)/shard_map/reduce_sum | solution.py:9
  441.9 0.0 copy-start.1
  441.9 0.2 fusion.5
  442.1 1.4 copy-done.1
  443.5 9.8 %convolution_subtract_fusion = f32[1024,1024]{1,0:T(8,128)} fusion(f32[1024,1024]{1,0:T(8,128)} %param.9, f32[1024,512]{1,0:T(8,128)S(1)} %copy-done.1, f32[1024,256]{1,0:T(8,128)S(1)} %get-tuple-element.4, f32[1024,256]{1,0:T(8,128)S(1)} %get-tuple-element.3), kind=kOutput, calls=%fused_computation | convolution fusion | flops 6444023808 | bytes 12582912 | tf_op jit(solution)/shard_map/dot_general | solution.py:13
Async XLA Ops:
  7.2 1.0 copy-start
  7.2 5.7 %copy-start.3 = (f32[64,256]{1,0:T(8,128)S(1)}, f32[64,256]{1,0:T(8,128)}, u32[]{:S(2)}) copy-start(f32[64,256]{1,0:T(8,128)} %param.8) | copy-start | bytes 196612
  7.2 45.0 %all-gather.4.cloned.1.call-start = ((), (), s32[]{:S(2)}) async-start(), calls=%async_computation | async-start | bytes 2228224 | tf_op jit(solution)/shard_map/all_gather | solution.py:26
  9.9 43.8 %copy-start.2 = (f32[256,256]{1,0:T(8,128)}, f32[256,256]{1,0:T(8,128)S(1)}, u32[]{:S(2)}) copy-start(f32[256,256]{1,0:T(8,128)S(1)} %fusion.8) | copy-start | bytes 786436
  13.6 415.6 %all-gather.6.cloned.1.call-start = ((), (), s32[]{:S(2)}) async-start(), calls=%async_computation.1 | async-start | bytes 35651584 | tf_op jit(solution)/shard_map/all_gather | solution.py:9
  441.9 1.6 copy-start.1
Sparse Core Ops, SparseCore 0:
  13.7 38.3 all-gather.3
  55.2 373.9 all-gather.5
